TPU v7x, 32 devices: a whole 2x2x4 slice. The times are simulated.
32 devices in a mesh: tp: 4 (over y, x), row: 4 (over z), col: 2 (over core).
Axes of the slice: x: 2, y: 2, z: 4, core: 2. Of those that a mesh axis runs over, the one named last changes fastest.
Arguments:
- hidden: bfloat16 [128, 14336], P('col', 'row'), may hold values from -6 to 6
- out_grad: bfloat16 [128, 4096], P(None, ('tp', 'row')), may hold values from -6 to 6
- basis_in: bfloat16 [14336, 4096], P(('row', 'col'), 'tp'), may hold values from -0.046875 to 0.046875
- basis_out: bfloat16 [4096, 1024], P(('tp', 'row'), 'col'), may hold values from -0.09375 to 0.09375
- eigen: float32 [4096, 1024], P(('tp', 'row'), 'col'), may hold values from 0.02 to 2
Outputs:
- precond: float32 [4096, 14336], P(('tp', 'col'), 'row')
All inputs are finite; a program needn't handle non-finite values.
Results may differ from a plain program's by a relative error of at most 0.024.
Values may be sent and summed in bfloat16 or wider, within the bound.
No kernel may reach another device: no remote copies, remote signals or barrier semaphores. Data moves between devices by JAX's collectives and lax.ppermute only.
A program may use at most 64 MiB of HBM per device.

v0:
```python
import jax
import jax.numpy as jnp
from jax import lax
from jax.sharding import PartitionSpec as P

damping = 0.01


def contract_rows(left, right):
    return lax.dot_general(
        left, right, (((0,), (0,)), ((), ())), preferred_element_type=jnp.float32
    )


def contract_cols(left, right):
    return lax.dot_general(
        left, right, (((1,), (1,)), ((), ())), preferred_element_type=jnp.float32
    )


def shards(hidden, out_grad, basis_in, basis_out, eigen):
    tp_count = lax.axis_size("tp")
    col_count = lax.axis_size("col")
    basis_block = lax.all_gather(basis_in, "col", axis=0, tiled=True)
    partial_in = jnp.dot(hidden, basis_block, preferred_element_type=jnp.float32)
    rotated_in = lax.psum_scatter(
        partial_in.astype(jnp.bfloat16), "row", scatter_dimension=1, tiled=True
    )
    rotated_in = lax.all_gather(rotated_in, "col", axis=0, tiled=True)
    queries = rotated_in.shape[0]
    partial_out = jnp.dot(out_grad, basis_out, preferred_element_type=jnp.float32)
    rotated_out = lax.psum(partial_out, ("tp", "row")).astype(jnp.bfloat16)
    coeff = contract_rows(rotated_in, rotated_out)
    scaled = (coeff / (queries * (eigen + damping))).astype(jnp.bfloat16)
    mixed_part = contract_cols(scaled, lax.all_gather(basis_out, ("tp", "row"), axis=0, tiled=True))
    depth = mixed_part.shape[0]
    width = mixed_part.shape[1]
    mixed_part = mixed_part.reshape(depth, tp_count, col_count, width // (tp_count * col_count))
    mixed = lax.psum_scatter(
        mixed_part.astype(jnp.bfloat16), "col", scatter_dimension=2, tiled=True
    ).astype(jnp.float32)
    mixed = mixed.reshape(depth, width // col_count).astype(jnp.bfloat16)
    mixed = lax.all_gather(mixed, "row", axis=0, tiled=True)
    return lax.psum_scatter(
        lax.dot_general(
            mixed, basis_block, (((0,), (1,)), ((), ())), preferred_element_type=jnp.float32
        ).astype(jnp.bfloat16),
        "tp",
        scatter_dimension=0,
        tiled=True,
    ).astype(jnp.float32)


def solution(mesh):
    placed = (
        P("col", "row"),
        P(None, ("tp", "row")),
        P(("row", "col"), "tp"),
        P(("tp", "row"), "col"),
        P(("tp", "row"), "col"),
    )
    return jax.shard_map(
        shards, mesh=mesh, in_specs=placed, out_specs=P(("tp", "col"), "row"), check_vma=False
    )
```

profile of v0, /device:TPU:0, one launch (start us, length us, event | category | flops | bytes accessed | tf_op | source)
XLA Modules:
  0.0 397.8 jit_solution(9604397828768367093)
XLA Ops:
  7.4 0.0 copy-start
  7.4 0.0 all-gather.4.cloned.1.call-start
  7.4 0.7 all-gather.4.cloned.1.call-update
  8.1 0.0 copy-start.1
  8.1 0.0 copy-start.2
  8.1 0.0 copy-start.3
  8.1 0.0 reduce-scatter.4.cloned.1.call-start
  8.2 22.6 %all-gather.4.cloned.1.call-done = bf16[3584,1024]{1,0:T(8,128)(2,1)} async-done(((bf16[1792,1024]{1,0:T(8,128)(2,1)}), bf16[3584,1024]{1,0:T(8,128)(2,1)}) %all-gather.4.cloned.1.call-update) | async-done | bytes 7340048 | tf_op jit(solution)/shard_map/all_gather | solution.py:24
  30.8 0.0 copy-done
  30.8 5.1 %convolution_convert_fusion.2 = bf16[64,1024]{1,0:T(8,128)(2,1)} fusion(bf16[64,3584]{1,0:T(8,128)(2,1)S(1)} %copy-done, bf16[3584,1024]{1,0:T(8,128)(2,1)} %all-gather.4.cloned.1.call-done), kind=kOutput, calls=%fused_computation.4 | convolution fusion | flops 469827584 | bytes 7929856 | tf_op jit(solution)/shard_map/dot_general | solution.py:25
  35.9 0.0 reduce-scatter.4.cloned.1.call-update
  35.9 0.0 all-gather.6.cloned.1.call-start
  36.0 0.5 all-gather.6.cloned.1.call-update
  36.5 0.0 reduce-scatter.6.cloned.1.call-start
  36.5 0.0 copy-done.1
  36.6 0.2 fusion.9
  36.8 85.1 %all-reduce.1 = bf16[128,512]{1,0:T(8,128)(2,1)S(1)} all-reduce(f32[128,512]{1,0:T(8,128)S(1)} %fusion.9), channel_id=1, replica_groups=mesh['tp'=4,'row'=4,'col'=2] {'tp','row'}, use_global_device_ids=true, to_apply=%region_1.0 | all-reduce | flops 65536 | bytes 393216 | tf_op jit(solution)/shard_map/psum | solution.py:32
  121.9 0.0 reduce-scatter.4.cloned.1.call-done
  121.9 2.1 all_gather.13
  124.0 4.9 %convolution_convert_fusion.1 = bf16[256,4096]{1,0:T(8,128)(2,1)} fusion(bf16[4096,512]{1,0:T(8,128)(2,1)} %all-gather.6.cloned.1.call-done, bf16[128,256]{1,0:T(8,128)(2,1)S(1)} %all_gather.13, f32[256,512]{1,0:T(8,128)S(1)} %copy-done.3, bf16[128,512]{1,0:T(8,128)(2,1)S(1)} %all-reduce.1), kind=kOutput, calls=%fused_computation.1 | convolution fusion | flops 1108869120 | bytes 7012352 | tf_op jit(solution)/shard_map/dot_general | solution.py:16
  128.9 3.3 convert_element_type.30
  132.2 4.1 %copy.6 = bf16[256,4,2,512]{0,3,1,2:T(8,128)(2,1)} copy(bf16[256,4,2,512]{3,2,1,0:T(2,128)(2,1)S(1)} %convert_element_type.30) | data formatting | bytes 4194304 | tf_op jit(solution)/shard_map/convert_element_type | solution.py:40
  136.3 0.0 reduce-scatter.6.cloned.1.call-update
  136.4 0.0 all-gather.8.cloned.1.call-start
  136.4 6.9 %reduce-scatter.6.cloned.1.call-done = bf16[256,4,1,512]{0,3,1,2:T(8,128)(2,1)} async-done(((bf16[256,4,2,512]{0,3,1,2:T(8,128)(2,1)}), bf16[256,4,1,512]{0,3,1,2:T(8,128)(2,1)}) %reduce-scatter.6.cloned.1.call-update) | async-done | bytes 1048592 | tf_op jit(solution)/shard_map/reduce_scatter | solution.py:39
  143.3 0.0 all-gather.8.cloned.1.call-update
  143.4 0.0 reduce-scatter.8.cloned.1.call-start
  143.4 83.2 %all-gather.8.cloned.1.call-done = bf16[1024,2048]{0,1:T(8,128)(2,1)} async-done(((bf16[256,2048]{0,1:T(8,128)(2,1)}), bf16[1024,2048]{0,1:T(8,128)(2,1)}) %all-gather.8.cloned.1.call-update) | async-done | bytes 4194320 | tf_op jit(solution)/shard_map/all_gather | solution.py:43
  226.6 22.0 %convolution_convert_fusion = bf16[2048,3584]{1,0:T(8,128)(2,1)} fusion(bf16[1024,2048]{0,1:T(8,128)(2,1)} %all-gather.8.cloned.1.call-done, bf16[3584,1024]{1,0:T(8,128)(2,1)} %all-gather.4.cloned.1.call-done), kind=kOutput, calls=%fused_computation | convolution fusion | flops 15039725568 | bytes 26214400 | tf_op jit(solution)/shard_map/dot_general | solution.py:45
  248.6 0.0 reduce-scatter.8.cloned.1.call-update
  248.7 135.9 %reduce-scatter.8.cloned.1.call-done = bf16[512,3584]{1,0:T(8,128)(2,1)} async-done(((bf16[2048,3584]{1,0:T(8,128)(2,1)}), bf16[512,3584]{1,0:T(8,128)(2,1)}) %reduce-scatter.8.cloned.1.call-update) | async-done | bytes 3670032 | tf_op jit(solution)/shard_map/reduce_scatter | solution.py:44
  384.6 6.0 %convert_element_type.33 = f32[512,3584]{1,0:T(8,128)} convert(bf16[512,3584]{1,0:T(8,128)(2,1)} %reduce-scatter.8.cloned.1.call-done) | non-fusion elementwise | flops 1835008 | bytes 11010048 | tf_op jit(solution)/shard_map/convert_element_type | solution.py:51
  (3 shorter events, 0.0 us)
Async XLA Ops:
  7.4 23.4 %copy-start = (bf16[64,3584]{1,0:T(8,128)(2,1)S(1)}, bf16[64,3584]{1,0:T(8,128)(2,1)}, u32[]{:S(2)}) copy-start(bf16[64,3584]{1,0:T(8,128)(2,1)} %param.5) | copy-start | bytes 1376260
  7.4 23.4 %all-gather.4.cloned.1.call-start = ((), (), s32[]{:S(2)}) async-start(), calls=%async_computation.3 | async-start | bytes 11010048 | tf_op jit(solution)/shard_map/all_gather | solution.py:24
  8.1 28.5 %copy-start.1 = (bf16[256,512]{1,0:T(8,128)(2,1)S(1)}, bf16[256,512]{1,0:T(8,128)(2,1)}, u32[]{:S(2)}) copy-start(bf16[256,512]{1,0:T(8,128)(2,1)} %param.8) | copy-start | bytes 786436
  8.1 28.5 %copy-start.2 = (bf16[128,256]{1,0:T(8,128)(2,1)S(1)}, bf16[128,256]{1,0:T(8,128)(2,1)}, u32[]{:S(2)}) copy-start(bf16[128,256]{1,0:T(8,128)(2,1)} %param.6) | copy-start | bytes 196612
  8.1 115.9 %copy-start.3 = (f32[256,512]{1,0:T(8,128)S(1)}, f32[256,512]{1,0:T(8,128)}, u32[]{:S(2)}) copy-start(f32[256,512]{1,0:T(8,128)} %param.9) | copy-start | bytes 1572868
  8.1 113.8 %reduce-scatter.4.cloned.1.call-start = ((), (), s32[]{:S(2)}) async-start(), calls=%async_computation.4 | async-start | bytes 163840 | tf_op jit(solution)/shard_map/reduce_scatter | solution.py:26
  35.9 88.1 %all-gather.6.cloned.1.call-start = ((), (), s32[]{:S(2)}) async-start(), calls=%async_computation.5 | async-start | bytes 4456448 | tf_op jit(solution)/shard_map/all_gather | solution.py:35
  36.5 106.8 %reduce-scatter.6.cloned.1.call-start = ((), (), s32[]{:S(2)}) async-start(), calls=%async_computation.6 | async-start | bytes 3145728 | tf_op jit(solution)/shard_map/reduce_scatter | solution.py:39
  136.4 90.2 %all-gather.8.cloned.1.call-start = ((), (), s32[]{:S(2)}) async-start(), calls=%async_computation.7 | async-start | bytes 5242880 | tf_op jit(solution)/shard_map/all_gather | solution.py:43
  143.4 241.2 %reduce-scatter.8.cloned.1.call-start = ((), (), s32[]{:S(2)}) async-start(), calls=%async_computation.8 | async-start | bytes 18350080 | tf_op jit(solution)/shard_map/reduce_scatter | solution.py:44
Sparse Core Ops, SparseCore 0:
  9.7 21.0 all-gather.3
  36.0 21.2 reduce-scatter.3
  136.5 6.8 reduce-scatter.5
  144.7 81.7 all-gather.7
Sparse Core Ops, SparseCore 1:
  39.2 78.1 all-gather.5
  248.7 135.8 reduce-scatter.7
where the time goes:
time: 398 us
  waiting for transfers between devices  250 us (63%)
  blocking collectives  87.2 us (22%)
  matrix products  32.3 us (8%)
  between operations  14.7 us (4%)
  local copies, waits for them, and re-layouts  7.4 us (2%)
  other arithmetic  6.04 us (2%)
    reduce_scatter x1, waiting for transfers between devices, shards(): lax.psum_scatter(lax.dot_general(mixed, basis_block, (((0,), (1,)), ((),...  136 us
    psum x1, blocking collectives, shards(): rotated_out = lax.psum(partial_out, ('tp', 'row')).astype(jnp.bfloat16)  85.1 us
    all_gather x1, waiting for transfers between devices, shards(): mixed = lax.all_gather(mixed, 'row', axis=0, tiled=True)  83.2 us
    all_gather x1, waiting for transfers between devices, shards(): basis_block = lax.all_gather(basis_in, 'col', axis=0, tiled=True)  22.6 us
    dot_general x1, matrix products, shards(): lax.dot_general(mixed, basis_block, (((0,), (1,)), ((), ())), preferred_e...  22 us
  transfers between devices with their start and end apart: 6, of which 4 were waited for; matrix products, arithmetic and copies ran while one was open for 0% of the time, Pallas kernels for 0%

commit v1 on v0

--- a/solution.py
+++ b/solution.py
@@ -29,7 +29,7 @@
     rotated_in = lax.all_gather(rotated_in, "col", axis=0, tiled=True)
     queries = rotated_in.shape[0]
     partial_out = jnp.dot(out_grad, basis_out, preferred_element_type=jnp.float32)
-    rotated_out = lax.psum(partial_out, ("tp", "row")).astype(jnp.bfloat16)
+    rotated_out = lax.psum(lax.psum(partial_out, "row"), "tp").astype(jnp.bfloat16)
     coeff = contract_rows(rotated_in, rotated_out)
     scaled = (coeff / (queries * (eigen + damping))).astype(jnp.bfloat16)
     mixed_part = contract_cols(scaled, lax.all_gather(basis_out, ("tp", "row"), axis=0, tiled=True))

time: 398 us -> 421 us (1.058)
  waiting for transfers between devices: 250 us -> 335 us
  blocking collectives: 87.2 us -> 22.9 us
    all_gather x1, waiting for transfers between devices: 0.01 us -> 74.3 us  [shards(): lax.all_gather(basis_out, ('tp', 'row'), axis=0, tiled=True)]
    psum x1, blocking collectives: 85.1 us -> 20.8 us  [shards(): lax.psum(lax.psum(partial_out, 'row'), 'tp').astype(jnp.bfloat16)]
    psum x0 -> x1, waiting for transfers between devices: none -> 12.6 us  [shards(): lax.psum(partial_out, 'row')]
  transfers between devices with their start and end apart: 6 -> 7, of which waited for: 4 -> 7; matrix products, arithmetic and copies ran while one was open for 0% -> 2% of each run, Pallas kernels for 0% -> 0%
where the time goes in v1:
time: 421 us
  waiting for transfers between devices  335 us (80%)
  matrix products  33.9 us (8%)
  blocking collectives  22.9 us (5%)
  between operations  14.9 us (4%)
  local copies, waits for them, and re-layouts  7.4 us (2%)
  other arithmetic  6.04 us (1%)
    reduce_scatter x1, waiting for transfers between devices, shards(): lax.psum_scatter(lax.dot_general(mixed, basis_block, (((0,), (1,)), ((),...  136 us
    all_gather x1, waiting for transfers between devices, shards(): mixed = lax.all_gather(mixed, 'row', axis=0, tiled=True)  81.7 us
    all_gather x1, waiting for transfers between devices, shards(): lax.all_gather(basis_out, ('tp', 'row'), axis=0, tiled=True)  74.3 us
    dot_general x1, matrix products, shards(): lax.dot_general(mixed, basis_block, (((0,), (1,)), ((), ())), preferred_e...  22 us
    psum x1, blocking collectives, shards(): lax.psum(lax.psum(partial_out, 'row'), 'tp').astype(jnp.bfloat16)  20.8 us
    all_gather x1, waiting for transfers between devices, shards(): basis_block = lax.all_gather(basis_in, 'col', axis=0, tiled=True)  20.7 us
    psum x1, waiting for transfers between devices, shards(): lax.psum(partial_out, 'row')  12.6 us
    reduce_scatter x1, waiting for transfers between devices, shards(): lax.psum_scatter(mixed_part.astype(jnp.bfloat16), 'col', scatter_dimensio...  8.46 us
  transfers between devices with their start and end apart: 7, of which 7 were waited for; matrix products, arithmetic and copies ran while one was open for 2% of the time, Pallas kernels for 0%

profile of v1, /device:TPU:0, one launch (start us, length us, event | category | flops | bytes accessed | tf_op | source)
XLA Modules:
  0.0 420.8 jit_solution(7065538336549004446)
XLA Ops:
  7.4 0.0 copy-start
  7.4 0.0 all-gather.4.cloned.1.call-start
  7.4 0.7 all-gather.4.cloned.1.call-update
  8.1 0.0 all-reduce.3.cloned.1.call-start
  8.1 1.9 fusion.9
  10.0 0.0 all-reduce.3.cloned.1.call-update
  10.0 0.0 copy-start.1
  10.1 0.0 reduce-scatter.4.cloned.1.call-start
  10.1 20.7 %all-gather.4.cloned.1.call-done = bf16[3584,1024]{1,0:T(8,128)(2,1)} async-done(((bf16[1792,1024]{1,0:T(8,128)(2,1)}), bf16[3584,1024]{1,0:T(8,128)(2,1)}) %all-gather.4.cloned.1.call-update) | async-done | bytes 7340048 | tf_op jit(solution)/shard_map/all_gather | solution.py:24
  30.8 5.1 %convolution_convert_fusion.2 = bf16[64,1024]{1,0:T(8,128)(2,1)} fusion(bf16[64,3584]{1,0:T(8,128)(2,1)S(1)} %copy-done, bf16[3584,1024]{1,0:T(8,128)(2,1)} %all-gather.4.cloned.1.call-done), kind=kOutput, calls=%fused_computation.4 | convolution fusion | flops 469827584 | bytes 7929856 | tf_op jit(solution)/shard_map/dot_general | solution.py:25
  35.9 0.0 reduce-scatter.4.cloned.1.call-update
  35.9 0.0 all-gather.6.cloned.1.call-start
  36.0 0.5 all-gather.6.cloned.1.call-update
  36.5 0.0 reduce-scatter.6.cloned.1.call-start
  36.6 12.6 %all-reduce.3.cloned.1.call-done = f32[128,512]{1,0:T(8,128)} async-done(((f32[128,512]{1,0:T(8,128)}), f32[128,512]{1,0:T(8,128)}) %all-reduce.3.cloned.1.call-update) | async-done | bytes 262160 | tf_op jit(solution)/shard_map/psum | solution.py:32
  49.2 20.8 %all-reduce.4 = bf16[128,512]{1,0:T(8,128)(2,1)S(1)} all-reduce(f32[128,512]{1,0:T(8,128)} %all-reduce.3.cloned.1.call-done), channel_id=1, replica_groups=mesh['tp'=4,'row'=4,'col'=2] {'tp'}, use_global_device_ids=true, to_apply=%region_2.0 | all-reduce | flops 65536 | bytes 393216 | tf_op jit(solution)/shard_map/psum | solution.py:32
  70.0 0.2 reduce-scatter.4.cloned.1.call-done
  70.3 2.1 all_gather.13
  72.3 74.3 %all-gather.6.cloned.1.call-done = bf16[4096,512]{1,0:T(8,128)(2,1)} async-done(((bf16[256,512]{1,0:T(8,128)(2,1)}), bf16[4096,512]{1,0:T(8,128)(2,1)}) %all-gather.6.cloned.1.call-update) | async-done | bytes 4194320 | tf_op jit(solution)/shard_map/all_gather | solution.py:35
  146.6 4.9 %convolution_convert_fusion.1 = bf16[256,4096]{1,0:T(8,128)(2,1)} fusion(bf16[4096,512]{1,0:T(8,128)(2,1)} %all-gather.6.cloned.1.call-done, bf16[128,256]{1,0:T(8,128)(2,1)S(1)} %all_gather.13, f32[256,512]{1,0:T(8,128)S(1)} %copy-done.1, bf16[128,512]{1,0:T(8,128)(2,1)S(1)} %all-reduce.4), kind=kOutput, calls=%fused_computation.1 | convolution fusion | flops 1108869120 | bytes 7012352 | tf_op jit(solution)/shard_map/dot_general | solution.py:16
  151.5 3.3 convert_element_type.30
  154.8 4.1 copy.6
  158.9 0.0 reduce-scatter.6.cloned.1.call-update
  158.9 0.0 all-gather.8.cloned.1.call-start
  159.0 8.5 %reduce-scatter.6.cloned.1.call-done = bf16[256,4,1,512]{0,3,1,2:T(8,128)(2,1)} async-done(((bf16[256,4,2,512]{0,3,1,2:T(8,128)(2,1)}), bf16[256,4,1,512]{0,3,1,2:T(8,128)(2,1)}) %reduce-scatter.6.cloned.1.call-update) | async-done | bytes 1048592 | tf_op jit(solution)/shard_map/reduce_scatter | solution.py:39
  167.5 0.0 all-gather.8.cloned.1.call-update
  167.5 0.0 reduce-scatter.8.cloned.1.call-start
  167.5 81.7 %all-gather.8.cloned.1.call-done = bf16[1024,2048]{0,1:T(8,128)(2,1)} async-done(((bf16[256,2048]{0,1:T(8,128)(2,1)}), bf16[1024,2048]{0,1:T(8,128)(2,1)}) %all-gather.8.cloned.1.call-update) | async-done | bytes 4194320 | tf_op jit(solution)/shard_map/all_gather | solution.py:43
  249.3 22.0 %convolution_convert_fusion = bf16[2048,3584]{1,0:T(8,128)(2,1)} fusion(bf16[1024,2048]{0,1:T(8,128)(2,1)} %all-gather.8.cloned.1.call-done, bf16[3584,1024]{1,0:T(8,128)(2,1)} %all-gather.4.cloned.1.call-done), kind=kOutput, calls=%fused_computation | convolution fusion | flops 15039725568 | bytes 26214400 | tf_op jit(solution)/shard_map/dot_general | solution.py:45
  271.3 0.0 reduce-scatter.8.cloned.1.call-update
  271.3 136.1 %reduce-scatter.8.cloned.1.call-done = bf16[512,3584]{1,0:T(8,128)(2,1)} async-done(((bf16[2048,3584]{1,0:T(8,128)(2,1)}), bf16[512,3584]{1,0:T(8,128)(2,1)}) %reduce-scatter.8.cloned.1.call-update) | async-done | bytes 3670032 | tf_op jit(solution)/shard_map/reduce_scatter | solution.py:44
  407.4 6.0 %convert_element_type.33 = f32[512,3584]{1,0:T(8,128)} convert(bf16[512,3584]{1,0:T(8,128)(2,1)} %reduce-scatter.8.cloned.1.call-done) | non-fusion elementwise | flops 1835008 | bytes 11010048 | tf_op jit(solution)/shard_map/convert_element_type | solution.py:51
  (2 shorter events, 0.0 us)
Async XLA Ops:
  7.4 23.4 %copy-start = (bf16[64,3584]{1,0:T(8,128)(2,1)S(1)}, bf16[64,3584]{1,0:T(8,128)(2,1)}, u32[]{:S(2)}) copy-start(bf16[64,3584]{1,0:T(8,128)(2,1)} %param.5) | copy-start | bytes 1376260
  7.4 23.4 %all-gather.4.cloned.1.call-start = ((), (), s32[]{:S(2)}) async-start(), calls=%async_computation.3 | async-start | bytes 11010048 | tf_op jit(solution)/shard_map/all_gather | solution.py:24
  8.1 41.1 %all-reduce.3.cloned.1.call-start = ((), (), s32[]{:S(2)}) async-start(), calls=%async_computation.5 | async-start | bytes 524288 | tf_op jit(solution)/shard_map/psum | solution.py:32
  10.0 136.5 %copy-start.1 = (f32[256,512]{1,0:T(8,128)S(1)}, f32[256,512]{1,0:T(8,128)}, u32[]{:S(2)}) copy-start(f32[256,512]{1,0:T(8,128)} %param.9) | copy-start | bytes 1572868
  10.1 60.2 %reduce-scatter.4.cloned.1.call-start = ((), (), s32[]{:S(2)}) async-start(), calls=%async_computation.4 | async-start | bytes 163840 | tf_op jit(solution)/shard_map/reduce_scatter | solution.py:26
  35.9 110.7 %all-gather.6.cloned.1.call-start = ((), (), s32[]{:S(2)}) async-start(), calls=%async_computation.6 | async-start | bytes 4456448 | tf_op jit(solution)/shard_map/all_gather | solution.py:35
  36.5 131.0 %reduce-scatter.6.cloned.1.call-start = ((), (), s32[]{:S(2)}) async-start(), calls=%async_computation.7 | async-start | bytes 3145728 | tf_op jit(solution)/shard_map/reduce_scatter | solution.py:39
  158.9 90.3 %all-gather.8.cloned.1.call-start = ((), (), s32[]{:S(2)}) async-start(), calls=%async_computation.8 | async-start | bytes 5242880 | tf_op jit(solution)/shard_map/all_gather | solution.py:43
  167.5 239.9 %reduce-scatter.8.cloned.1.call-start = ((), (), s32[]{:S(2)}) async-start(), calls=%async_computation.9 | async-start | bytes 18350080 | tf_op jit(solution)/shard_map/reduce_scatter | solution.py:44
Sparse Core Ops, SparseCore 0:
  9.7 21.0 all-gather.3
  159.1 8.3 reduce-scatter.5
  271.4 135.9 reduce-scatter.7
Sparse Core Ops, SparseCore 1:
  10.9 38.2 all-reduce.2
  51.3 18.9 reduce-scatter.3
  72.9 73.6 all-gather.5
  167.6 81.6 all-gather.7
